TPU v7x, 128 devices: a whole 4x4x4 slice. The times are simulated.
128 devices in a mesh: dom: 8 (over z, core), grp: 16 (over x, y).
Axes of the slice: x: 4, y: 4, z: 4, core: 2. Of those that a mesh axis runs over, the one named last changes fastest.
Arguments:
- src_table: float32 [16384, 400], P(('dom', 'grp')), may hold values from -8 to 8
- src_state: float32 [16384], P(('dom', 'grp')), may hold values from 0.01 to 1
- tgt_table: float32 [131072, 400], P(('dom', 'grp')), may hold values from -8 to 8
- tgt_state: float32 [131072], P(('dom', 'grp')), may hold values from 0.01 to 1
- pair_source: int32 [2, 131072], P(None, ('dom', 'grp')), may hold values from 0 to 127
- pair_owner: int32 [2, 131072, 1], P(None, ('dom', 'grp')), may hold values from 0 to 15; in each aligned block of 1024 rows (0 to 1023, 1024 to 2047, ..., all dimensions but the last counted through in order) at most 256 rows name the same one
- pair_offset: int32 [2, 131072], P(None, ('dom', 'grp')), may hold values from 0 to 1023
- negatives: int32 [8, 1000], P('dom'), may hold values from 0 to 16383
- plan: int32 [2, 8], replicated, may hold values from 0 to 7, each once within a row
Outputs:
- src_trained: float32 [16384, 400], P(('dom', 'grp'))
- src_accum: float32 [16384], P(('dom', 'grp'))
- tgt_trained: float32 [131072, 400], P(('dom', 'grp'))
- tgt_accum: float32 [131072], P(('dom', 'grp'))
Inputs may be any that keep to these rules, and one draw needn't show every extreme that they name: `pair_owner`: in every round the pairs of one device name each owner at most 256 times, and some device's pairs name some owner exactly 256 times. `plan`: each round's row names every dom index once.
All inputs are finite; a program needn't handle non-finite values.
Results may differ from a plain program's by a relative error of at most 0.011.
Values may be sent and summed in bfloat16 or wider, within the bound.
No kernel may reach another device: no remote copies, remote signals or barrier semaphores. Data moves between devices by JAX's collectives and lax.ppermute only.
A program may use at most 128 MiB of HBM per device.

v0:
```python
import jax
import jax.numpy as jnp
from jax import lax
from jax.sharding import PartitionSpec as P

LEARN = 0.1


def adagrad(emb_table, opt_state, grads):
    new_state = opt_state + jnp.mean(grads * grads, axis=1)
    return (emb_table - LEARN * grads / jnp.sqrt(new_state)[:, None], new_state)


def slot_holding(sched_row, wanted):
    return jnp.sum(
        jnp.arange(sched_row.shape[0], dtype=jnp.int32) * (sched_row == wanted).astype(jnp.int32)
    )


def relayout(emb_table, opt_state, want_slot):
    carried = (jnp.zeros_like(emb_table), jnp.zeros_like(opt_state))
    pieces = (
        lax.all_gather(emb_table, "dom", axis=0, tiled=True),
        lax.all_gather(opt_state, "dom", axis=0, tiled=True),
    )
    row_count = carried[0].shape[0]
    row_total = pieces[0].shape[0]
    local_index = jnp.arange(row_count, dtype=jnp.int32) + want_slot * row_count
    is_inside = (local_index >= 0) & (local_index < row_total)
    safe_index = jnp.clip(local_index, 0, row_total - 1)
    new_rows = jnp.where(is_inside[:, None], jnp.take(pieces[0], safe_index, axis=0), carried[0])
    new_state = jnp.where(is_inside, jnp.take(pieces[1], safe_index, axis=0), carried[1])
    return (new_rows, new_state)


def train_round(
    held_table, held_state, tgt_table, tgt_state, sources, owners, offsets, neg_ids, my_grp
):
    group_count = lax.axis_size("grp")
    src_count, emb_width = held_table.shape
    tgt_count = tgt_table.shape[0]
    pair_count = sources.shape[0]
    capacity = pair_count // 4
    slot_count = group_count * capacity
    owned_ids = neg_ids - my_grp * tgt_count
    is_mine = (owned_ids >= 0) & (owned_ids < tgt_count)
    owned_safe = jnp.clip(owned_ids, 0, tgt_count - 1)
    src_bf = held_table.astype(jnp.bfloat16)
    tgt_bf = tgt_table.astype(jnp.bfloat16)
    local_rows = jnp.where(is_mine[:, None], jnp.take(tgt_table, owned_safe, axis=0), 0.0)
    neg_rows = lax.psum(local_rows, "grp").astype(jnp.bfloat16)
    dest_onehot = (owners[:, None] == jnp.arange(group_count, dtype=jnp.int32)[None, :]).astype(
        jnp.int32
    )
    slot_rank = jnp.sum((jnp.cumsum(dest_onehot, axis=0) - 1) * dest_onehot, axis=1)
    slot_place = owners * capacity + slot_rank
    out_offsets = jnp.full((slot_count,), -1, jnp.int32).at[slot_place].set(offsets)
    outgoing = (
        jnp.zeros((slot_count, emb_width), jnp.bfloat16)
        .at[slot_place]
        .set(jnp.take(src_bf, sources, axis=0))
    )
    incoming, got_offsets = (
        lax.all_to_all(
            outgoing.reshape(group_count, capacity, emb_width),
            "grp",
            split_axis=0,
            concat_axis=0,
            tiled=True,
        ),
        lax.all_to_all(
            out_offsets.reshape(group_count, capacity),
            "grp",
            split_axis=0,
            concat_axis=0,
            tiled=True,
        ),
    )
    incoming = incoming.reshape(slot_count, emb_width)
    got_offsets = got_offsets.reshape(slot_count)
    is_valid = (got_offsets >= 0).astype(jnp.float32)
    safe_offsets = jnp.clip(got_offsets, 0, tgt_count - 1)
    target_rows = jnp.take(tgt_bf, safe_offsets, axis=0)
    positive = jnp.einsum("sd,sd->s", incoming, target_rows, preferred_element_type=jnp.float32)
    negative = lax.dot_general(
        incoming, neg_rows, (((1,), (1,)), ((), ())), preferred_element_type=jnp.float32
    )
    score_max = jnp.maximum(jnp.max(negative, axis=1), positive)
    pos_exp = jnp.exp(positive - score_max)
    neg_exp = jnp.exp(negative - score_max[:, None])
    exp_total = pos_exp + jnp.sum(neg_exp, axis=1)
    d_pos = (pos_exp / exp_total - 1.0) * is_valid
    d_neg = (neg_exp / exp_total[:, None] * is_valid[:, None]).astype(jnp.bfloat16)
    source_grad = (
        d_pos[:, None] * target_rows.astype(jnp.float32)
        + jnp.dot(d_neg, neg_rows, preferred_element_type=jnp.float32)
    ).astype(jnp.bfloat16)
    returned = lax.all_to_all(
        source_grad.reshape(group_count, capacity, emb_width),
        "grp",
        split_axis=0,
        concat_axis=0,
        tiled=True,
    ).reshape(slot_count, emb_width)
    pair_grad = jnp.take(returned, slot_place, axis=0).astype(jnp.float32)
    src_grads = jnp.zeros((src_count, emb_width), jnp.float32).at[sources].add(pair_grad)
    tgt_grads = (
        jnp.zeros((tgt_count, emb_width), jnp.float32)
        .at[safe_offsets]
        .add(d_pos[:, None] * incoming.astype(jnp.float32))
    )
    neg_part = lax.dot_general(
        d_neg, incoming, (((0,), (0,)), ((), ())), preferred_element_type=jnp.float32
    )
    summed = lax.psum(neg_part, "grp")
    tgt_grads = tgt_grads.at[owned_safe].add(jnp.where(is_mine[:, None], summed, 0.0))
    held_table, held_state = adagrad(held_table, held_state, src_grads)
    tgt_table, tgt_state = adagrad(tgt_table, tgt_state, tgt_grads)
    return (held_table, held_state, tgt_table, tgt_state)


def shards(
    src_table,
    src_state,
    tgt_table,
    tgt_state,
    pair_source,
    pair_owner,
    pair_offset,
    negatives,
    plan,
):
    my_dom = lax.axis_index("dom")
    my_grp = lax.axis_index("grp")
    round_count = plan.shape[0]
    neg_ids = negatives[0]
    for round_index in range(round_count):
        held_table, held_state = relayout(src_table, src_state, plan[round_index, my_dom])
        held_table, held_state, tgt_table, tgt_state = train_round(
            held_table,
            held_state,
            tgt_table,
            tgt_state,
            pair_source[round_index],
            pair_owner[round_index, :, 0],
            pair_offset[round_index],
            neg_ids,
            my_grp,
        )
        src_table, src_state = relayout(
            held_table, held_state, slot_holding(plan[round_index], my_dom)
        )
    return (src_table, src_state, tgt_table, tgt_state)


def solution(mesh):
    return jax.shard_map(
        shards,
        mesh=mesh,
        in_specs=(
            P(("dom", "grp"), None),
            P(("dom", "grp")),
            P(("dom", "grp"), None),
            P(("dom", "grp")),
            P(None, ("dom", "grp")),
            P(None, ("dom", "grp"), None),
            P(None, ("dom", "grp")),
            P("dom", None),
            P(),
        ),
        out_specs=(
            P(("dom", "grp"), None),
            P(("dom", "grp")),
            P(("dom", "grp"), None),
            P(("dom", "grp")),
        ),
        check_vma=False,
    )
```

profile of v0, /device:TPU:1, one launch (start us, length us, event | category | flops | bytes accessed | tf_op | source)
XLA Modules:
  0.0 816.0 jit_solution(2772978685348490794)
XLA Ops:
  27.2 7.6 all-to-all-start
  42.0 13.0 %scatter_custom_fusion.1 = bf16[4096,400]{1,0:T(8,128)(2,1)} fusion(s32[1024]{0:T(1024)S(1)} %bitcast.168, bf16[]{:T(256)} %constant.84.clone.1, pred[1024]{0:T(1024)(128)(4,1)S(1)} %compare_and_fusion.6, bf16[]{:T(256)} %constant.29.clone.2, bf16[128,400]{1,0:T(8,128)(2,1)S(1)} %fusion.38, s32[1024]{0:T(1024)S(1)} %fusion.56), kind=kCustom, calls=%fused_computation.58 | custom fusion | flops 409600 | bytes 3412996 | tf_op jit(solution)/shard_map/scatter | solution.py:61
  83.4 97.5 %all-reduce.8 = bf16[1000,400]{0,1:T(8,128)(2,1)} all-reduce(f32[1000,400]{0,1:T(8,128)S(1)} %select_select_fusion.1), channel_id=1, replica_groups=mesh['dom'=8,'grp'=16] {'grp'}, use_global_device_ids=true, to_apply=%region_7.12 | all-reduce | flops 400000 | bytes 2400000 | tf_op jit(solution)/shard_map/psum | solution.py:51
  181.1 17.3 %gather_fusion.1 = bf16[4096,400]{1,0:T(8,128)(2,1)} fusion(bf16[1024,400]{1,0:T(8,128)(2,1)S(1)} %copy.82, s32[4096]{0:T(1024)S(1)} %fusion.48), kind=kCustom, calls=%fused_computation.2.clone | custom fusion | bytes 6569984 | tf_op jit(solution)/shard_map/jit(_take)/gather | solution.py:83
  206.9 8.0 fusion.77
  216.1 7.9 fusion
  224.0 7.6 multiply_convert_fusion.1
  242.8 21.5 %all-gather = f32[8,1,128]{2,1,0:T(1,128)S(1)} all-gather(f32[1,1,128]{2,1,0:T(1,128)S(1)} %bitcast.173), channel_id=1, replica_groups=mesh['dom'=8,'grp'=16] {'dom'}, dimensions={0}, use_global_device_ids=true | all-gather | bytes 4608 | tf_op jit(solution)/shard_map/all_gather | solution.py:24
  276.0 15.2 %scatter_custom_fusion.2 = f32[128,400]{1,0:T(8,128)} fusion(s32[1024]{0:T(1024)} %bitcast.169, pred[1024]{0:T(1024)(128)(4,1)} %compare_and_fusion.4, bf16[]{:T(256)} %constant.29.clone.2, f32[]{:T(128)} %constant.60.clone.1, bf16[4096,400]{1,0:T(8,128)(2,1)} %bitcast.126, s32[1024]{0:T(1024)} %broadcast_clamp_fusion.3), kind=kCustom, calls=%fused_computation.54 | custom fusion | flops 1228800 | bytes 4405248 | tf_op jit(solution)/shard_map/scatter-add | solution.py:106
  300.1 16.7 %all-to-all-start.3 = ((s32[16,1,256]{2,1,0:T(1,128)}), s32[16,1,256]{2,1,0:T(1,128)}, u32[]{:S(2)}, u32[]{:S(2)}) async-start(s32[16,1,256]{2,1,0:T(1,128)} %bitcast.32), calls=%async_computation.3 | async-start | bytes 32768 | tf_op jit(solution)/shard_map/all_to_all | solution.py:71
  324.4 11.6 %all-gather.11.cloned.1.call-done = f32[1024,400]{1,0:T(8,128)} async-done(((f32[128,400]{1,0:T(8,128)}), f32[1024,400]{1,0:T(8,128)}) %all-gather.11.cloned.1.call-update) | async-done | bytes 1638416 | tf_op jit(solution)/shard_map/all_gather | solution.py:23
  344.6 7.2 fusion.79
  352.4 13.7 %all-gather.13.cloned.1.call-done = f32[1024,400]{1,0:T(8,128)} async-done(((f32[128,400]{1,0:T(8,128)}), f32[1024,400]{1,0:T(8,128)}) %all-gather.13.cloned.1.call-update) | async-done | bytes 1638416 | tf_op jit(solution)/shard_map/all_gather | solution.py:23
  370.1 15.9 %scatter_custom_fusion.4 = bf16[4096,400]{1,0:T(8,128)(2,1)} fusion(s32[1024]{0:T(1024)} %bitcast.164, bf16[]{:T(256)} %constant.84.clone.1, pred[1024]{0:T(1024)(128)(4,1)S(1)} %copy-done.40, bf16[]{:T(256)} %constant.29.clone.2, bf16[128,400]{1,0:T(8,128)(2,1)} %fusion.39, s32[1024]{0:T(1024)S(1)} %copy-done.32), kind=kCustom, calls=%fused_computation.56 | custom fusion | flops 409600 | bytes 3414016 | tf_op jit(solution)/shard_map/scatter | solution.py:61
  392.0 6.8 all-to-all-start.4
  403.2 8.5 %copy.92 = f32[4096,400]{1,0:T(8,128)} copy(f32[4096,400]{0,1:T(8,128)} %convert_multiply_fusion.2) | data formatting | bytes 13107200 | tf_op jit(solution)/shard_map/mul | solution.py:110
  411.7 29.3 %scatter_custom_fusion.5 = f32[1024,400]{1,0:T(8,128)S(1)} fusion(s32[4096]{0:T(1024)} %bitcast.161, f32[4096,400]{1,0:T(8,128)} %copy.92, f32[]{:T(128)} %constant.60.clone.1), kind=kCustom, calls=%fused_computation.68 | custom fusion | flops 1638400 | bytes 1638912 | tf_op jit(solution)/shard_map/scatter-add | solution.py:110
  441.0 48.3 %all-reduce.5.cloned.1.call-done = f32[1000,400]{0,1:T(8,128)} async-done(((f32[1000,400]{0,1:T(8,128)}), f32[1000,400]{0,1:T(8,128)}) %all-reduce.5.cloned.1.call-update) | async-done | bytes 1600016 | tf_op jit(solution)/shard_map/psum | solution.py:115
  495.0 8.7 %scatter_fusion = f32[1024,400]{1,0:T(8,128)S(1)} fusion(f32[1024,400]{1,0:T(8,128)S(1)} %scatter_custom_fusion.5, s32[1000]{0:T(1024)S(1)} %bitcast.151, f32[1000,400]{1,0:T(8,128)} %copy.93), kind=kCustom, calls=%fused_computation.22 | custom fusion | flops 400000 | bytes 4804000 | tf_op jit(solution)/shard_map/scatter-add | solution.py:116
  516.2 17.3 %gather_fusion.6 = bf16[4096,400]{1,0:T(8,128)(2,1)} fusion(bf16[1024,400]{1,0:T(8,128)(2,1)S(1)} %get-tuple-element.32, s32[4096]{0:T(1024)S(1)} %copy-done.16), kind=kCustom, calls=%fused_computation.10.clone | custom fusion | bytes 6569984 | tf_op jit(solution)/shard_map/jit(_take)/gather | solution.py:83
  539.5 73.8 %all-reduce.9 = bf16[1000,400]{0,1:T(8,128)(2,1)} all-reduce(f32[1000,400]{0,1:T(8,128)S(1)} %select_select_fusion), channel_id=1, replica_groups=mesh['dom'=8,'grp'=16] {'grp'}, use_global_device_ids=true, to_apply=%region_21.28 | all-reduce | flops 400000 | bytes 2400000 | tf_op jit(solution)/shard_map/psum | solution.py:51
  615.7 8.0 fusion.78
  625.0 7.9 fusion.1
  632.9 7.6 multiply_convert_fusion
  652.2 7.2 fusion.80
  661.8 28.2 %all-gather.1 = f32[8,1,128]{2,1,0:T(1,128)S(1)} all-gather(f32[1,1,128]{2,1,0:T(1,128)} %bitcast.171), channel_id=1, replica_groups=mesh['dom'=8,'grp'=16] {'dom'}, dimensions={0}, use_global_device_ids=true | all-gather | bytes 4608 | tf_op jit(solution)/shard_map/all_gather | solution.py:24
  692.3 8.5 %all-gather.2 = f32[8,1,128]{2,1,0:T(1,128)S(1)} all-gather(f32[1,1,128]{2,1,0:T(1,128)S(1)} %fusion.62), channel_id=1, replica_groups=mesh['dom'=8,'grp'=16] {'dom'}, dimensions={0}, use_global_device_ids=true | all-gather | bytes 4608 | tf_op jit(solution)/shard_map/all_gather | solution.py:24
  708.4 15.0 %scatter_custom_fusion.7 = f32[128,400]{1,0:T(8,128)} fusion(s32[1024]{0:T(1024)} %bitcast.165, pred[1024]{0:T(1024)(128)(4,1)S(1)} %copy-done.41, bf16[]{:T(256)} %constant.29.clone.2, f32[]{:T(128)} %constant.60.clone.1, bf16[4096,400]{1,0:T(8,128)(2,1)} %bitcast.125, s32[1024]{0:T(1024)S(1)} %copy-done.31), kind=kCustom, calls=%fused_computation.50 | custom fusion | flops 1228800 | bytes 4405248 | tf_op jit(solution)/shard_map/scatter-add | solution.py:106
  732.1 8.6 %copy.99 = f32[4096,400]{1,0:T(8,128)} copy(f32[4096,400]{0,1:T(8,128)} %convert_multiply_fusion) | data formatting | bytes 13107200 | tf_op jit(solution)/shard_map/mul | solution.py:110
  740.6 29.4 %scatter_custom_fusion.8 = f32[1024,400]{1,0:T(8,128)S(1)} fusion(s32[4096]{0:T(1024)S(1)} %bitcast.162, f32[4096,400]{1,0:T(8,128)} %copy.99, f32[]{:T(128)} %constant.60.clone.1), kind=kCustom, calls=%fused_computation.66 | custom fusion | flops 1638400 | bytes 1638912 | tf_op jit(solution)/shard_map/scatter-add | solution.py:110
  776.1 8.8 %scatter_fusion.1 = f32[1024,400]{1,0:T(8,128)S(1)} fusion(f32[1024,400]{1,0:T(8,128)S(1)} %scatter_custom_fusion.8, s32[1000]{0:T(1024)S(1)} %bitcast.152, f32[1000,400]{1,0:T(8,128)} %copy.100), kind=kCustom, calls=%fused_computation.25 | custom fusion | flops 400000 | bytes 4804000 | tf_op jit(solution)/shard_map/scatter-add | solution.py:116
  791.1 12.7 %all-gather.3 = f32[8,1,128]{2,1,0:T(1,128)S(1)} all-gather(f32[1,1,128]{2,1,0:T(1,128)S(1)} %bitcast.172), channel_id=1, replica_groups=mesh['dom'=8,'grp'=16] {'dom'}, dimensions={0}, use_global_device_ids=true | all-gather | bytes 4608 | tf_op jit(solution)/shard_map/all_gather | solution.py:24
  (248 shorter events, 203.1 us)
Async XLA Ops:
  7.2 32.2 %all-gather.9.cloned.1.call-start = ((), (), s32[]{:S(2)}) async-start(), calls=%async_computation.6 | async-start | bytes 2359296 | tf_op jit(solution)/shard_map/all_gather | solution.py:23
  9.7 28.6 %copy-start.14 = (s32[1,1024,1]{1,2,0:T(1,128)}, s32[1,1024,1]{1,2,0:T(1,128)S(1)}, u32[]{:S(2)}) copy-start(s32[1,1024,1]{1,2,0:T(1,128)S(1)} %get-tuple-element.49) | copy-start | bytes 12292
  19.5 18.8 %copy-start.19 = (s32[1024]{0:T(1024)}, s32[1024]{0:T(1024)S(1)}, u32[]{:S(2)}) copy-start(s32[1024]{0:T(1024)S(1)} %fusion.43) | copy-start | bytes 12292
  27.2 33.8 %all-to-all-start = ((s32[16,1,256]{2,1,0:T(1,128)}), s32[16,1,256]{2,1,0:T(1,128)S(1)}, u32[]{:S(2)}, u32[]{:S(2)}) async-start(s32[16,1,256]{2,1,0:T(1,128)} %bitcast.14), calls=%async_computation | async-start | bytes 32768 | tf_op jit(solution)/shard_map/all_to_all | solution.py:71
  36.9 18.1 %copy-start.43 = (pred[128]{0:T(512)(128)(4,1)}, pred[128]{0:T(512)(128)(4,1)S(1)}, u32[]{:S(2)}) copy-start(pred[128]{0:T(512)(128)(4,1)S(1)} %get-tuple-element.58) | copy-start | bytes 388
  36.9 18.1 %copy-start.44 = (pred[128]{0:T(512)(128)(4,1)}, pred[128]{0:T(512)(128)(4,1)S(1)}, u32[]{:S(2)}) copy-start(pred[128]{0:T(512)(128)(4,1)S(1)} %get-tuple-element.59) | copy-start | bytes 388
  41.8 19.2 %copy-start.9 = (f32[128,400]{1,0:T(8,128)}, f32[128,400]{1,0:T(8,128)S(1)}, u32[]{:S(2)}) copy-start(f32[128,400]{1,0:T(8,128)S(1)} %gather_fusion) | copy-start | bytes 614404
  61.1 143.3 %all-to-all-start.1 = ((bf16[16,256,400]{1,2,0:T(8,128)(2,1)}), bf16[16,256,400]{1,2,0:T(8,128)(2,1)}, u32[]{:S(2)}, u32[]{:S(2)}) async-start(bf16[16,256,400]{1,2,0:T(8,128)(2,1)} %copy.80), calls=%async_computation.1 | async-start | bytes 6553600 | tf_op jit(solution)/shard_map/all_to_all | solution.py:64
  238.1 28.9 %copy-start.27 = (s32[2,1024]{1,0:T(2,128)S(1)}, s32[2,1024]{1,0:T(2,128)}, u32[]{:S(2)}) copy-start(s32[2,1024]{1,0:T(2,128)} %param.25) | copy-start | bytes 24580
  238.1 31.9 %all-to-all-start.2 = ((bf16[16,256,400]{1,2,0:T(8,128)(2,1)}), bf16[16,256,400]{1,2,0:T(8,128)(2,1)}, u32[]{:S(2)}, u32[]{:S(2)}) async-start(bf16[16,256,400]{1,2,0:T(8,128)(2,1)} %bitcast.130), calls=%async_computation.2 | async-start | bytes 6553600 | tf_op jit(solution)/shard_map/all_to_all | solution.py:98
  242.7 93.3 %all-gather.11.cloned.1.call-start = ((), (), s32[]{:S(2)}) async-start(), calls=%async_computation.7 | async-start | bytes 2359296 | tf_op jit(solution)/shard_map/all_gather | solution.py:23
  276.0 17.3 %copy-start.10 = (f32[128,400]{1,0:T(8,128)S(1)}, f32[128,400]{1,0:T(8,128)}, u32[]{:S(2)}) copy-start(f32[128,400]{1,0:T(8,128)} %copy-done.9) | copy-start | bytes 614404
  300.1 40.5 %all-to-all-start.3 = ((s32[16,1,256]{2,1,0:T(1,128)}), s32[16,1,256]{2,1,0:T(1,128)}, u32[]{:S(2)}, u32[]{:S(2)}) async-start(s32[16,1,256]{2,1,0:T(1,128)} %bitcast.32), calls=%async_computation.3 | async-start | bytes 32768 | tf_op jit(solution)/shard_map/all_to_all | solution.py:71
  316.8 49.3 %all-gather.13.cloned.1.call-start = ((), (), s32[]{:S(2)}) async-start(), calls=%async_computation.8 | async-start | bytes 2359296 | tf_op jit(solution)/shard_map/all_gather | solution.py:23
  340.1 149.2 %all-reduce.5.cloned.1.call-start = ((), (), s32[]{:S(2)}) async-start(), calls=%async_computation.9 | async-start | bytes 3276800 | tf_op jit(solution)/shard_map/psum | solution.py:115
  343.3 8.4 %copy-start.13 = (s32[16,1,256]{2,1,0:T(1,128)}, s32[16,1,256]{2,1,0:T(1,128)S(1)}, u32[]{:S(2)}) copy-start(s32[16,1,256]{2,1,0:T(1,128)S(1)} %broadcast_clamp_fusion) | copy-start | bytes 49156
  351.7 16.9 %copy-start.42 = (pred[128]{0:T(512)(128)(4,1)S(1)}, pred[128]{0:T(512)(128)(4,1)}, u32[]{:S(2)}) copy-start(pred[128]{0:T(512)(128)(4,1)} %get-tuple-element.62) | copy-start | bytes 388
  351.7 18.3 %copy-start.32 = (s32[1024]{0:T(1024)S(1)}, s32[1024]{0:T(1024)}, u32[]{:S(2)}) copy-start(s32[1024]{0:T(1024)} %fusion.57) | copy-start | bytes 12292
  351.7 18.3 %copy-start.40 = (pred[1024]{0:T(1024)(128)(4,1)S(1)}, pred[1024]{0:T(1024)(128)(4,1)}, u32[]{:S(2)}) copy-start(pred[1024]{0:T(1024)(128)(4,1)} %compare_and_fusion.3) | copy-start | bytes 3076
  392.0 221.3 %all-to-all-start.4 = ((bf16[16,256,400]{1,2,0:T(8,128)(2,1)}), bf16[16,256,400]{1,2,0:T(8,128)(2,1)}, u32[]{:S(2)}, u32[]{:S(2)}) async-start(bf16[16,256,400]{1,2,0:T(8,128)(2,1)} %copy.90), calls=%async_computation.4 | async-start | bytes 6553600 | tf_op jit(solution)/shard_map/all_to_all | solution.py:64
  403.2 86.2 %copy-start.29 = (pred[1000]{0:T(1024)(128)(4,1)S(1)}, pred[1000]{0:T(1024)(128)(4,1)}, u32[]{:S(2)}) copy-start(pred[1000]{0:T(1024)(128)(4,1)} %copy-done.28) | copy-start | bytes 3004
  441.0 54.0 %copy-start.22 = (s32[1000,1]{0,1:T(1,128)S(1)}, s32[1000,1]{0,1:T(1,128)}, u32[]{:S(2)}) copy-start(s32[1000,1]{0,1:T(1,128)} %get-tuple-element.34) | copy-start | bytes 12004
  495.0 8.9 %copy-start.33 = (f32[1024]{0:T(1024)S(1)}, f32[1024]{0:T(1024)}, u32[]{:S(2)}) copy-start(f32[1024]{0:T(1024)} %param.24) | copy-start | bytes 12292
  646.9 55.5 %all-to-all-start.5 = ((bf16[16,256,400]{1,2,0:T(8,128)(2,1)}), bf16[16,256,400]{1,2,0:T(8,128)(2,1)}, u32[]{:S(2)}, u32[]{:S(2)}) async-start(bf16[16,256,400]{1,2,0:T(8,128)(2,1)} %bitcast.129), calls=%async_computation.5 | async-start | bytes 6553600 | tf_op jit(solution)/shard_map/all_to_all | solution.py:98
  651.4 119.0 %all-reduce.7.cloned.1.call-start = ((), (), s32[]{:S(2)}) async-start(), calls=%async_computation.11 | async-start | bytes 3276800 | tf_op jit(solution)/shard_map/psum | solution.py:115
  652.1 8.5 %copy-start.15 = (s32[1,1024,1]{1,2,0:T(1,128)S(1)}, s32[1,1024,1]{1,2,0:T(1,128)}, u32[]{:S(2)}) copy-start(s32[1,1024,1]{1,2,0:T(1,128)} %copy-done.14) | copy-start | bytes 12292
  652.2 8.5 %copy-start.20 = (s32[1024]{0:T(1024)S(1)}, s32[1024]{0:T(1024)}, u32[]{:S(2)}) copy-start(s32[1024]{0:T(1024)} %copy-done.19) | copy-start | bytes 12292
  659.4 146.1 %all-gather.15.cloned.1.call-start = ((), (), s32[]{:S(2)}) async-start(), calls=%async_computation.10 | async-start | bytes 2359296 | tf_op jit(solution)/shard_map/all_gather | solution.py:23
  732.1 38.4 %copy-start.30 = (pred[1000]{0:T(1024)(128)(4,1)S(1)}, pred[1000]{0:T(1024)(128)(4,1)}, u32[]{:S(2)}) copy-start(pred[1000]{0:T(1024)(128)(4,1)} %copy-done.28) | copy-start | bytes 3004
  776.1 9.1 %copy-start.34 = (f32[1024]{0:T(1024)S(1)}, f32[1024]{0:T(1024)}, u32[]{:S(2)}) copy-start(f32[1024]{0:T(1024)} %param.24) | copy-start | bytes 12292
  788.3 19.7 %copy-start.46 = (pred[128]{0:T(512)(128)(4,1)S(1)}, pred[128]{0:T(512)(128)(4,1)}, u32[]{:S(2)}) copy-start(pred[128]{0:T(512)(128)(4,1)} %get-tuple-element.64) | copy-start | bytes 388
  788.3 19.7 %copy-start.47 = (pred[128]{0:T(512)(128)(4,1)S(1)}, pred[128]{0:T(512)(128)(4,1)}, u32[]{:S(2)}) copy-start(pred[128]{0:T(512)(128)(4,1)} %get-tuple-element.65) | copy-start | bytes 388
  (28 other events, 134.6 us)
Sparse Core Ops, SparseCore 0:
  10.3 29.0 all-gather.8
  295.2 40.8 all-gather.10
  340.3 25.7 all-gather.12
  369.8 119.4 all-reduce.4
  659.5 110.9 all-reduce.6
  772.0 26.9 all-gather.14
where the time goes:
time: 828 us; the launch traced here: 816 us
  blocking collectives  242 us (29%)
  other arithmetic  231 us (28%)
  local copies, waits for them, and re-layouts  160 us (19%)
  waiting for transfers between devices  77.6 us (9%)
  starting transfers between devices  47.5 us (6%)
  matrix products  39.2 us (5%)
  between operations  17.8 us (2%)
    psum x2, blocking collectives, train_round(): neg_rows = lax.psum(local_rows, 'grp').astype(jnp.bfloat16)  171 us
    all_gather x4, blocking collectives, relayout(): lax.all_gather(opt_state, 'dom', axis=0, tiled=True)  71 us
    scatter-add x2, other arithmetic, train_round(): tgt_grads = jnp.zeros((tgt_count, emb_width), jnp.float32).at[safe_offset...  58.7 us
    psum x2, waiting for transfers between devices, train_round(): summed = lax.psum(neg_part, 'grp')  48.7 us
    gather x4, local copies, waits for them, and re-layouts, train_round(): target_rows = jnp.take(tgt_bf, safe_offsets, axis=0)  46.6 us
    scatter-add x2, other arithmetic, train_round(): jnp.zeros((src_count, emb_width), jnp.float32).at[sources].add(pair_grad)  30.2 us
    scatter x2, other arithmetic, train_round(): outgoing = jnp.zeros((slot_count, emb_width), jnp.bfloat16).at[slot_place...  28.9 us
    all_gather x4, waiting for transfers between devices, relayout(): lax.all_gather(emb_table, 'dom', axis=0, tiled=True)  26.4 us
  transfers between devices with their start and end apart: 12, of which 6 were waited for; matrix products, arithmetic and copies ran while one was open for 40% of the time, Pallas kernels for 0%

commit v1 on v0

--- a/solution.py
+++ b/solution.py
@@ -4,6 +4,11 @@
 from jax.sharding import PartitionSpec as P
 
 LEARN = 0.1
+
+
+def summed_here(array, axis):
+    terms = lax.all_gather(array, axis)
+    return jnp.sum(terms, axis=0)
 
 
 def adagrad(emb_table, opt_state, grads):
@@ -112,7 +117,7 @@
     neg_part = lax.dot_general(
         d_neg, incoming, (((0,), (0,)), ((), ())), preferred_element_type=jnp.float32
     )
-    summed = lax.psum(neg_part, "grp")
+    summed = summed_here(neg_part, "grp")
     tgt_grads = tgt_grads.at[owned_safe].add(jnp.where(is_mine[:, None], summed, 0.0))
     held_table, held_state = adagrad(held_table, held_state, src_grads)
     tgt_table, tgt_state = adagrad(tgt_table, tgt_state, tgt_grads)

time: 828 us -> 1040 us (1.26)
  waiting for transfers between devices: 77.6 us -> 290 us
    all_gather x0 -> x2, waiting for transfers between devices: none -> 228 us  [summed_here(): terms = lax.all_gather(array, axis)]
    psum x2 -> x0, waiting for transfers between devices: 48.7 us -> none  [train_round(): summed = lax.psum(neg_part, 'grp')]
    all_gather x4, waiting for transfers between devices: 26.4 us -> 48.6 us  [relayout(): lax.all_gather(emb_table, 'dom', axis=0, tiled=True)]
    reduce_sum x0 -> x2, other arithmetic: none -> 20.9 us  [summed_here(): return jnp.sum(terms, axis=0)]
    all_to_all x2, waiting for transfers between devices: 0.01 us -> 11.5 us  [train_round(): lax.all_to_all(outgoing.reshape(group_count, capacity, emb_width), 'grp',...]
  transfers between devices with their start and end apart: 12 -> 12, of which waited for: 6 -> 7; matrix products, arithmetic and copies ran while one was open for 40% -> 22% of each run, Pallas kernels for 0% -> 0%
where the time goes in v1:
time: 1040 us; the launch traced here: 1030 us
  waiting for transfers between devices  290 us (28%)
  blocking collectives  249 us (24%)
  other arithmetic  240 us (23%)
  local copies, waits for them, and re-layouts  153 us (15%)
  matrix products  42.6 us (4%)
  starting transfers between devices  37.6 us (4%)
  between operations  17.8 us (2%)
    all_gather x2, waiting for transfers between devices, summed_here(): terms = lax.all_gather(array, axis)  228 us
    psum x2, blocking collectives, train_round(): neg_rows = lax.psum(local_rows, 'grp').astype(jnp.bfloat16)  177 us
    all_gather x4, blocking collectives, relayout(): lax.all_gather(opt_state, 'dom', axis=0, tiled=True)  71.8 us
    scatter-add x2, other arithmetic, train_round(): tgt_grads = jnp.zeros((tgt_count, emb_width), jnp.float32).at[safe_offset...  60.5 us
    all_gather x4, waiting for transfers between devices, relayout(): lax.all_gather(emb_table, 'dom', axis=0, tiled=True)  48.6 us
    gather x4, local copies, waits for them, and re-layouts, train_round(): target_rows = jnp.take(tgt_bf, safe_offsets, axis=0)  46.7 us
    scatter-add x2, other arithmetic, train_round(): jnp.zeros((src_count, emb_width), jnp.float32).at[sources].add(pair_grad)  29.4 us
    scatter x2, other arithmetic, train_round(): outgoing = jnp.zeros((slot_count, emb_width), jnp.bfloat16).at[slot_place...  26.2 us
  transfers between devices with their start and end apart: 12, of which 7 were waited for; matrix products, arithmetic and copies ran while one was open for 22% of the time, Pallas kernels for 0%

profile of v1, /device:TPU:1, one launch (start us, length us, event | category | flops | bytes accessed | tf_op | source)
XLA Modules:
  0.0 1030.0 jit_solution(5021832760488997402)
XLA Ops:
  26.1 7.6 all-to-all-start
  41.9 13.0 %scatter_custom_fusion.1 = bf16[4096,400]{1,0:T(8,128)(2,1)} fusion(s32[1024]{0:T(1024)S(1)} %bitcast.172, bf16[]{:T(256)} %constant.84.clone.1, pred[1024]{0:T(1024)(128)(4,1)S(1)} %compare_and_fusion.6, bf16[]{:T(256)} %constant.29.clone.2, bf16[128,400]{1,0:T(8,128)(2,1)S(1)} %fusion.46, s32[1024]{0:T(1024)S(1)} %fusion.64), kind=kCustom, calls=%fused_computation.58 | custom fusion | flops 409600 | bytes 3412996 | tf_op jit(solution)/shard_map/scatter | solution.py:66
  82.2 98.9 %all-reduce.2 = bf16[1000,400]{1,0:T(8,128)(2,1)} all-reduce(f32[1000,400]{1,0:T(8,128)} %select_select_fusion.1), channel_id=1, replica_groups=mesh['dom'=8,'grp'=16] {'grp'}, use_global_device_ids=true, to_apply=%region_7.12 | all-reduce | flops 400000 | bytes 2400000 | tf_op jit(solution)/shard_map/psum | solution.py:56
  181.3 17.3 %gather_fusion.1 = bf16[4096,400]{1,0:T(8,128)(2,1)} fusion(bf16[1024,400]{1,0:T(8,128)(2,1)S(1)} %copy.74, s32[4096]{0:T(1024)S(1)} %fusion.56), kind=kCustom, calls=%fused_computation.2.clone | custom fusion | bytes 6569984 | tf_op jit(solution)/shard_map/jit(_take)/gather | solution.py:88
  207.1 8.0 fusion.85
  216.3 7.9 fusion
  224.2 7.6 multiply_convert_fusion.1
  243.0 22.6 %all-gather.2 = f32[8,1,128]{2,1,0:T(1,128)S(1)} all-gather(f32[1,1,128]{2,1,0:T(1,128)S(1)} %bitcast.177), channel_id=1, replica_groups=mesh['dom'=8,'grp'=16] {'dom'}, dimensions={0}, use_global_device_ids=true | all-gather | bytes 4608 | tf_op jit(solution)/shard_map/all_gather | solution.py:29
  275.5 14.3 %scatter_custom_fusion.2 = f32[128,400]{1,0:T(8,128)S(1)} fusion(s32[1024]{0:T(1024)S(1)} %bitcast.173, pred[1024]{0:T(1024)(128)(4,1)S(1)} %compare_and_fusion.4, bf16[]{:T(256)} %constant.29.clone.2, f32[]{:T(128)} %constant.60.clone.1, bf16[4096,400]{1,0:T(8,128)(2,1)} %bitcast.130, s32[1024]{0:T(1024)S(1)} %broadcast_clamp_fusion.3), kind=kCustom, calls=%fused_computation.54 | custom fusion | flops 1228800 | bytes 3486726 | tf_op jit(solution)/shard_map/scatter-add | solution.py:111
  292.8 41.5 %all-gather.17.cloned.1.call-done = f32[1024,400]{1,0:T(8,128)} async-done(((f32[128,400]{1,0:T(8,128)}), f32[1024,400]{1,0:T(8,128)}) %all-gather.17.cloned.1.call-update) | async-done | bytes 1638416 | tf_op jit(solution)/shard_map/all_gather | solution.py:28
  337.7 9.0 convolution_bitcast_fusion.1
  366.1 13.2 %scatter_custom_fusion.4 = bf16[4096,400]{1,0:T(8,128)(2,1)} fusion(s32[1024]{0:T(1024)S(1)} %bitcast.168, bf16[]{:T(256)} %constant.84.clone.1, pred[1024]{0:T(1024)(128)(4,1)S(1)} %compare_and_fusion.3, bf16[]{:T(256)} %constant.29.clone.2, bf16[128,400]{1,0:T(8,128)(2,1)S(1)} %fusion.47, s32[1024]{0:T(1024)S(1)} %fusion.65), kind=kCustom, calls=%fused_computation.56 | custom fusion | flops 409600 | bytes 3412996 | tf_op jit(solution)/shard_map/scatter | solution.py:66
  399.3 8.5 copy.83
  407.8 30.2 %scatter_custom_fusion.5 = f32[1024,400]{1,0:T(8,128)} fusion(s32[4096]{0:T(1024)S(1)} %bitcast.163, f32[4096,400]{1,0:T(8,128)} %copy.83, f32[]{:T(128)} %constant.60.clone.1), kind=kCustom, calls=%fused_computation.74 | custom fusion | flops 1638400 | bytes 1638912 | tf_op jit(solution)/shard_map/scatter-add | solution.py:115
  437.9 11.5 %all-to-all-done.4 = bf16[16,256,400]{1,2,0:T(8,128)(2,1)} async-done(((bf16[16,256,400]{1,2,0:T(8,128)(2,1)}), bf16[16,256,400]{1,2,0:T(8,128)(2,1)}, u32[]{:S(2)}, u32[]{:S(2)}) %all-to-all-start.4) | async-done | bytes 3276832 | tf_op jit(solution)/shard_map/all_to_all | solution.py:69
  454.5 104.0 %all-gather.23.cloned.1.call-done = f32[16,1000,400]{1,2,0:T(8,128)} async-done(((f32[1,1000,400]{1,2,0:T(8,128)}), f32[16,1000,400]{1,2,0:T(8,128)}) %all-gather.23.cloned.1.call-update) | async-done | bytes 25600016 | tf_op jit(solution)/shard_map/all_gather | solution.py:10
  558.5 11.0 %reduce_sum.120 = f32[1000,400]{0,1:T(8,128)} reduce(f32[16,1000,400]{1,2,0:T(8,128)} %all-gather.23.cloned.1.call-done, f32[]{:T(128)} %constant.60.clone.1), dimensions={0}, to_apply=%region_18.25 | reduce | flops 6000000 | bytes 27200004 | tf_op jit(solution)/shard_map/reduce_sum | solution.py:11
  572.3 11.9 %scatter_custom_fusion.6 = f32[1024,400]{1,0:T(8,128)} fusion(f32[1024,400]{1,0:T(8,128)} %scatter_custom_fusion.5, s32[1000]{0:T(1024)} %bitcast.165, f32[1000,400]{1,0:T(8,128)} %copy.84, f32[]{:T(128)} %constant.60.clone.1, pred[1000]{0:T(1024)(128)(4,1)S(1)} %and_reduce_fusion), kind=kCustom, calls=%fused_computation.64 | custom fusion | flops 800000 | bytes 3687912 | tf_op jit(solution)/shard_map/scatter-add | solution.py:121
  595.7 78.0 %all-reduce.3 = bf16[1000,400]{1,0:T(8,128)(2,1)} all-reduce(f32[1000,400]{1,0:T(8,128)} %select_select_fusion), channel_id=1, replica_groups=mesh['dom'=8,'grp'=16] {'grp'}, use_global_device_ids=true, to_apply=%region_21.28 | all-reduce | flops 400000 | bytes 2400000 | tf_op jit(solution)/shard_map/psum | solution.py:56
  673.7 17.3 %gather_fusion.6 = bf16[4096,400]{1,0:T(8,128)(2,1)} fusion(bf16[1024,400]{1,0:T(8,128)(2,1)S(1)} %get-tuple-element.32, s32[4096]{0:T(1024)S(1)} %fusion.57), kind=kCustom, calls=%fused_computation.10.clone | custom fusion | bytes 6569984 | tf_op jit(solution)/shard_map/jit(_take)/gather | solution.py:88
  697.1 9.3 fusion.86
  707.7 7.9 fusion.1
  715.6 7.9 multiply_convert_fusion
  735.4 23.1 %all-gather.4 = f32[8,1,128]{2,1,0:T(1,128)S(1)} all-gather(f32[1,1,128]{2,1,0:T(1,128)} %bitcast.175), channel_id=1, replica_groups=mesh['dom'=8,'grp'=16] {'dom'}, dimensions={0}, use_global_device_ids=true | all-gather | bytes 4608 | tf_op jit(solution)/shard_map/all_gather | solution.py:29
  760.9 8.5 all-gather.5
  777.1 15.0 %scatter_custom_fusion.7 = f32[128,400]{1,0:T(8,128)} fusion(s32[1024]{0:T(1024)} %bitcast.169, pred[1024]{0:T(1024)(128)(4,1)S(1)} %copy-done.38, bf16[]{:T(256)} %constant.29.clone.2, f32[]{:T(128)} %constant.60.clone.1, bf16[4096,400]{1,0:T(8,128)(2,1)} %bitcast.129, s32[1024]{0:T(1024)S(1)} %broadcast_clamp_fusion.2), kind=kCustom, calls=%fused_computation.50 | custom fusion | flops 1228800 | bytes 4405248 | tf_op jit(solution)/shard_map/scatter-add | solution.py:111
  807.3 8.5 copy.89
  815.8 30.3 %scatter_custom_fusion.8 = f32[1024,400]{1,0:T(8,128)} fusion(s32[4096]{0:T(1024)S(1)} %bitcast.164, f32[4096,400]{1,0:T(8,128)} %copy.89, f32[]{:T(128)} %constant.60.clone.1), kind=kCustom, calls=%fused_computation.72 | custom fusion | flops 1638400 | bytes 1638912 | tf_op jit(solution)/shard_map/scatter-add | solution.py:115
  846.1 17.6 %all-gather.6 = f32[8,1,128]{2,1,0:T(1,128)S(1)} all-gather(f32[1,1,128]{2,1,0:T(1,128)S(1)} %bitcast.176), channel_id=1, replica_groups=mesh['dom'=8,'grp'=16] {'dom'}, dimensions={0}, use_global_device_ids=true | all-gather | bytes 4608 | tf_op jit(solution)/shard_map/all_gather | solution.py:29
  868.5 123.5 %all-gather.25.cloned.1.call-done = f32[16,1000,400]{1,2,0:T(8,128)} async-done(((f32[1,1000,400]{1,2,0:T(8,128)}), f32[16,1000,400]{1,2,0:T(8,128)}) %all-gather.25.cloned.1.call-update) | async-done | bytes 25600016 | tf_op jit(solution)/shard_map/all_gather | solution.py:10
  992.1 9.9 reduce_sum.124
  1003.8 12.1 %scatter_custom_fusion.9 = f32[1024,400]{1,0:T(8,128)} fusion(f32[1024,400]{1,0:T(8,128)} %scatter_custom_fusion.8, s32[1000]{0:T(1024)} %bitcast.166, f32[1000,400]{1,0:T(8,128)} %copy.90, f32[]{:T(128)} %constant.60.clone.1, pred[1000]{0:T(1024)(128)(4,1)S(1)} %copy-done.29), kind=kCustom, calls=%fused_computation.62 | custom fusion | flops 800000 | bytes 3687912 | tf_op jit(solution)/shard_map/scatter-add | solution.py:121
  (236 shorter events, 205.4 us)
Async XLA Ops:
  7.2 32.2 %all-gather.15.cloned.1.call-start = ((), (), s32[]{:S(2)}) async-start(), calls=%async_computation.6 | async-start | bytes 2359296 | tf_op jit(solution)/shard_map/all_gather | solution.py:28
  9.7 45.2 %copy-start.17 = (s32[1,1024,1]{1,2,0:T(1,128)}, s32[1,1024,1]{1,2,0:T(1,128)S(1)}, u32[]{:S(2)}) copy-start(s32[1,1024,1]{1,2,0:T(1,128)S(1)} %get-tuple-element.49) | copy-start | bytes 12292
  19.5 35.4 %copy-start.23 = (s32[1024]{0:T(1024)}, s32[1024]{0:T(1024)S(1)}, u32[]{:S(2)}) copy-start(s32[1024]{0:T(1024)S(1)} %fusion.51) | copy-start | bytes 12292
  26.1 35.0 %all-to-all-start = ((s32[16,1,256]{2,1,0:T(1,128)}), s32[16,1,256]{2,1,0:T(1,128)S(1)}, u32[]{:S(2)}, u32[]{:S(2)}) async-start(s32[16,1,256]{2,1,0:T(1,128)} %bitcast.14), calls=%async_computation | async-start | bytes 32768 | tf_op jit(solution)/shard_map/all_to_all | solution.py:76
  61.0 143.5 %all-to-all-start.1 = ((bf16[16,256,400]{1,2,0:T(8,128)(2,1)}), bf16[16,256,400]{1,2,0:T(8,128)(2,1)}, u32[]{:S(2)}, u32[]{:S(2)}) async-start(bf16[16,256,400]{1,2,0:T(8,128)(2,1)} %copy.72), calls=%async_computation.1 | async-start | bytes 6553600 | tf_op jit(solution)/shard_map/all_to_all | solution.py:69
  77.5 494.8 %copy-start.27 = (pred[1000]{0:T(1024)(128)(4,1)}, pred[1000]{0:T(1024)(128)(4,1)S(1)}, u32[]{:S(2)}) copy-start(pred[1000]{0:T(1024)(128)(4,1)S(1)} %and_reduce_fusion) | copy-start | bytes 3004
  77.5 103.6 %copy-start.34 = (pred[1000]{0:T(1024)(128)(4,1)}, pred[1000]{0:T(1024)(128)(4,1)S(1)}, u32[]{:S(2)}) copy-start(pred[1000]{0:T(1024)(128)(4,1)S(1)} %compare_and_fusion.5) | copy-start | bytes 3004
  181.2 23.3 %copy-start.13 = (s32[16,1,256]{2,1,0:T(1,128)}, s32[16,1,256]{2,1,0:T(1,128)S(1)}, u32[]{:S(2)}) copy-start(s32[16,1,256]{2,1,0:T(1,128)S(1)} %broadcast_clamp_fusion.1) | copy-start | bytes 49156
  207.0 8.0 copy-start.1
  238.3 28.3 %copy-start.26 = (s32[2,1024]{1,0:T(2,128)S(1)}, s32[2,1024]{1,0:T(2,128)}, u32[]{:S(2)}) copy-start(s32[2,1024]{1,0:T(2,128)} %param.25) | copy-start | bytes 24580
  238.3 31.2 %all-to-all-start.2 = ((bf16[16,256,400]{1,2,0:T(8,128)(2,1)}), bf16[16,256,400]{1,2,0:T(8,128)(2,1)}, u32[]{:S(2)}, u32[]{:S(2)}) async-start(bf16[16,256,400]{1,2,0:T(8,128)(2,1)} %bitcast.134), calls=%async_computation.2 | async-start | bytes 6553600 | tf_op jit(solution)/shard_map/all_to_all | solution.py:103
  243.0 91.4 %all-gather.17.cloned.1.call-start = ((), (), s32[]{:S(2)}) async-start(), calls=%async_computation.7 | async-start | bytes 2359296 | tf_op jit(solution)/shard_map/all_gather | solution.py:28
  275.5 16.0 %copy-start.39 = (s32[2,8]{1,0:T(2,128)S(1)}, s32[2,8]{1,0:T(2,128)}, u32[]{:S(2)}) copy-start(s32[2,8]{1,0:T(2,128)} %param.29) | copy-start | bytes 196
  291.4 72.1 %all-gather.19.cloned.1.call-start = ((), (), s32[]{:S(2)}) async-start(), calls=%async_computation.8 | async-start | bytes 2359296 | tf_op jit(solution)/shard_map/all_gather | solution.py:28
  292.8 53.9 %copy-start.36 = (s32[1024]{0:T(1024)}, s32[1024]{0:T(1024)S(1)}, u32[]{:S(2)}) copy-start(s32[1024]{0:T(1024)S(1)} %pad_clamp_fusion.2) | copy-start | bytes 12292
  337.6 220.9 %all-gather.23.cloned.1.call-start = ((), (), s32[]{:S(2)}) async-start(), calls=%async_computation.10 | async-start | bytes 27852800 | tf_op jit(solution)/shard_map/all_gather | solution.py:10
  351.6 33.9 %all-to-all-start.3 = ((s32[16,1,256]{2,1,0:T(1,128)}), s32[16,1,256]{2,1,0:T(1,128)S(1)}, u32[]{:S(2)}, u32[]{:S(2)}) async-start(s32[16,1,256]{2,1,0:T(1,128)} %bitcast.32), calls=%async_computation.3 | async-start | bytes 32768 | tf_op jit(solution)/shard_map/all_to_all | solution.py:76
  359.2 20.0 %copy-start.40 = (pred[128]{0:T(512)(128)(4,1)}, pred[128]{0:T(512)(128)(4,1)S(1)}, u32[]{:S(2)}) copy-start(pred[128]{0:T(512)(128)(4,1)S(1)} %get-tuple-element.62) | copy-start | bytes 388
  359.2 20.0 %copy-start.41 = (pred[128]{0:T(512)(128)(4,1)}, pred[128]{0:T(512)(128)(4,1)S(1)}, u32[]{:S(2)}) copy-start(pred[128]{0:T(512)(128)(4,1)S(1)} %get-tuple-element.63) | copy-start | bytes 388
  385.5 8.3 copy-start.14
  385.5 8.3 copy-start.20
  385.5 64.0 %all-to-all-start.4 = ((bf16[16,256,400]{1,2,0:T(8,128)(2,1)}), bf16[16,256,400]{1,2,0:T(8,128)(2,1)}, u32[]{:S(2)}, u32[]{:S(2)}) async-start(bf16[16,256,400]{1,2,0:T(8,128)(2,1)} %copy.81), calls=%async_computation.4 | async-start | bytes 6553600 | tf_op jit(solution)/shard_map/all_to_all | solution.py:69
  572.3 13.9 %copy-start.30 = (f32[1024]{0:T(1024)S(1)}, f32[1024]{0:T(1024)}, u32[]{:S(2)}) copy-start(f32[1024]{0:T(1024)} %param.24) | copy-start | bytes 12292
  697.1 9.3 copy-start.7
  697.1 9.4 copy-start.33
  730.2 40.9 %all-to-all-start.5 = ((bf16[16,256,400]{1,2,0:T(8,128)(2,1)}), bf16[16,256,400]{1,2,0:T(8,128)(2,1)}, u32[]{:S(2)}, u32[]{:S(2)}) async-start(bf16[16,256,400]{1,2,0:T(8,128)(2,1)} %bitcast.133), calls=%async_computation.5 | async-start | bytes 6553600 | tf_op jit(solution)/shard_map/all_to_all | solution.py:103
  734.8 130.3 %all-gather.21.cloned.1.call-start = ((), (), s32[]{:S(2)}) async-start(), calls=%async_computation.9 | async-start | bytes 2359296 | tf_op jit(solution)/shard_map/all_gather | solution.py:28
  795.7 8.1 copy-start.16
  795.7 8.1 copy-start.22
  795.7 196.4 %all-gather.25.cloned.1.call-start = ((), (), s32[]{:S(2)}) async-start(), calls=%async_computation.11 | async-start | bytes 27852800 | tf_op jit(solution)/shard_map/all_gather | solution.py:10
  1003.8 14.0 %copy-start.31 = (f32[1024]{0:T(1024)S(1)}, f32[1024]{0:T(1024)}, u32[]{:S(2)}) copy-start(f32[1024]{0:T(1024)} %param.24) | copy-start | bytes 12292
  1003.8 14.7 %copy-start = (f32[1024,400]{1,0:T(8,128)S(1)}, f32[1024,400]{1,0:T(8,128)}, u32[]{:S(2)}) copy-start(f32[1024,400]{1,0:T(8,128)} %get-tuple-element.33) | copy-start | bytes 4915204
  (23 other events, 128.1 us)
Sparse Core Ops, SparseCore 0:
  10.3 29.0 all-gather.14
  291.5 42.7 all-gather.16
  337.7 25.7 all-gather.18
  366.1 192.3 all-gather.22
  795.8 34.6 all-gather.20
  833.0 158.9 all-gather.24
